TPU v7x, 32 devices: a whole 2x2x4 slice. The times are simulated.
32 devices in a mesh: ctx: 8 (over z, x), ch: 4 (over y, core).
Axes of the slice: x: 2, y: 2, z: 4, core: 2. Of those that a mesh axis runs over, the one named last changes fastest.
Arguments:
- tokens: bfloat16 [2048, 4096], P('ctx', 'ch'), may hold values from -6 to 6
- in_weight: bfloat16 [4096, 3, 4096], P('ch', None, 'ctx'), may hold values from -0.09375 to 0.09375
- short_filter: float32 [4096, 3, 3], P('ch'), may hold values from -3 to 3
- decay_rates: float32 [4096, 16], P('ch'), may hold values from 0.00024414062 to 0.05
- residues: float32 [4096, 16], P('ch'), may hold values from -1.5 to 1.5
- skip_gain: float32 [4096], P('ch'), may hold values from -4 to 4
- out_weight: bfloat16 [4096, 4096], P(None, 'ch'), may hold values from -0.09375 to 0.09375
Outputs:
- mixed: bfloat16 [2048, 4096], P('ctx', 'ch')
All inputs are finite; a program needn't handle non-finite values.
Results may differ from a plain program's by a relative error of at most 0.02.
Values may be sent and summed in bfloat16 or wider, within the bound.
A program may use at most 320 MiB of HBM per device.

v0:
```python
import jax
import jax.numpy as jnp
from jax import lax
from jax.sharding import PartitionSpec as P

HIGHEST = lax.Precision.HIGHEST


def shifted(x, axis, by):
    size = lax.axis_size(axis)
    pairs = [(i, i + by) for i in range(size) if 0 <= i + by < size]
    return lax.ppermute(x, axis, pairs)


def local_conv(product, decay_rates, residues, span):
    chans, length = product.shape
    blocks = length // span
    mode_gain = residues * jnp.sqrt(-jnp.expm1(-2.0 * decay_rates))
    offsets = jnp.arange(span).astype(jnp.float32)
    falling = mode_gain[:, :, None] * jnp.exp(-decay_rates[:, :, None] * offsets)
    rising = jnp.exp(decay_rates[:, :, None] * offsets)
    toeplitz = jnp.einsum("cnt,cns->cts", falling, rising, precision=HIGHEST)
    lower = offsets[:, None] >= offsets[None, :]
    toeplitz = jnp.where(lower[None], toeplitz, 0.0)
    carry_in = mode_gain[:, :, None] * jnp.exp(-decay_rates[:, :, None] * (offsets + 1.0))
    carry_out = jnp.exp(-decay_rates[:, :, None] * (span - 1.0 - offsets))
    through = jnp.exp(-decay_rates * span)
    pieces = product.reshape(chans, blocks, span).transpose(1, 0, 2).astype(jnp.float32)
    within = jnp.einsum("cts,bcs->bct", toeplitz, pieces, precision=HIGHEST)
    injected = jnp.einsum("cns,bcs->bcn", carry_out, pieces, precision=HIGHEST)

    def advance(state, added):
        return (through * state + added, state)

    state, before = lax.scan(advance, jnp.zeros(decay_rates.shape, jnp.float32), injected)
    results = within + jnp.einsum("cnt,bcn->bct", carry_in, before, precision=HIGHEST)
    return (results.transpose(1, 0, 2).reshape(chans, length), state)


def local(tokens, in_weight, short_filter, decay_rates, residues, skip_gain, out_weight):
    rows_here = tokens.shape[0]
    terms = jnp.einsum(
        "rd,dsc->csr",
        tokens,
        lax.all_gather(in_weight, "ctx", axis=2, tiled=True),
        preferred_element_type=jnp.float32,
    )
    projected = lax.psum_scatter(terms.astype(jnp.bfloat16), "ch", scatter_dimension=0, tiled=True)
    group = projected.shape[0]
    reach = short_filter.shape[2] - 1
    rim = shifted(projected[:, :, rows_here - reach :], "ctx", 1)
    extended = jnp.concatenate([rim, projected], axis=2)
    featured = jnp.zeros(projected.shape, jnp.float32)
    for shift_by in range(reach + 1):
        begin = reach - shift_by
        featured = featured + short_filter[:, :, shift_by, None] * extended[
            :, :, begin : begin + rows_here
        ].astype(jnp.float32)
    query = featured[:, 0]
    product = (featured[:, 1] * featured[:, 2]).astype(jnp.bfloat16)
    count = lax.axis_size("ctx")
    chans = group // count
    sent = product.reshape(count, chans, rows_here)
    whole = lax.all_to_all(sent, "ctx", split_axis=0, concat_axis=2, tiled=True)
    length = whole.shape[2]
    start = lax.axis_index("ctx") * chans
    mine_rates = lax.dynamic_slice_in_dim(decay_rates, start, chans, 0)
    mine_residues = lax.dynamic_slice_in_dim(residues, start, chans, 0)
    full_out, final_state = local_conv(
        whole.reshape(chans, length), mine_rates, mine_residues, min(512, length)
    )
    back = lax.all_to_all(
        full_out.reshape(1, chans, length).astype(jnp.bfloat16),
        "ctx",
        split_axis=2,
        concat_axis=0,
        tiled=True,
    ).astype(jnp.float32)
    convolved = back.reshape(group, rows_here)
    gated = (query * (convolved + skip_gain[:, None] * product.astype(jnp.float32))).astype(
        jnp.bfloat16
    )
    mixed = lax.dot_general(
        lax.all_gather(gated, "ch", axis=0, tiled=True),
        out_weight,
        (((0,), (0,)), ((), ())),
        preferred_element_type=jnp.float32,
    )
    return mixed.astype(jnp.bfloat16)


def solution(mesh):
    in_specs = (
        P("ctx", "ch"),
        P("ch", None, "ctx"),
        P("ch", None, None),
        P("ch", None),
        P("ch", None),
        P("ch"),
        P(None, "ch"),
    )
    out_specs = P("ctx", "ch")
    return jax.shard_map(local, mesh=mesh, in_specs=in_specs, out_specs=out_specs, check_vma=False)
```

profile of v0, /device:TPU:1, one launch (start us, length us, event | category | flops | bytes accessed | tf_op | source)
XLA Modules:
  0.0 851.8 jit_solution(11152898393615489229)
XLA Ops:
  6.5 4.7 copy.22
  11.3 0.0 all-gather.3.cloned.1.call-update
  11.3 0.0 reduce-scatter.2.cloned.1.call-start
  11.3 482.6 %all-gather.3.cloned.1.call-done = bf16[1024,3,4096]{0,2,1:T(8,128)(2,1)} async-done(((bf16[1024,3,512]{0,2,1:T(8,128)(2,1)}), bf16[1024,3,4096]{0,2,1:T(8,128)(2,1)}) %all-gather.3.cloned.1.call-update) | async-done | bytes 25165840 | tf_op jit(solution)/shard_map/all_gather | solution.py:45
  494.0 13.3 %fusion.4 = bf16[4096,3,256]{2,0,1:T(8,128)(2,1)} fusion(bf16[1024,3,4096]{0,2,1:T(8,128)(2,1)} %all-gather.3.cloned.1.call-done, bf16[256,1024]{1,0:T(8,128)(2,1)S(1)} %copy-done), kind=kOutput, calls=%fused_computation.7 | convolution fusion | flops 6445596672 | bytes 31981568 | tf_op jit(solution)/shard_map/rd,dsc->csr/dot_general | solution.py:42
  507.3 0.0 reduce-scatter.2.cloned.1.call-update
  507.3 0.7 multiply_exponential_fusion
  508.0 0.7 sqrt_multiply_fusion
  508.8 57.0 %reduce-scatter.2.cloned.1.call-done = bf16[1024,3,256]{2,0,1:T(8,128)(2,1)} async-done(((bf16[4096,3,256]{2,0,1:T(8,128)(2,1)}), bf16[1024,3,256]{2,0,1:T(8,128)(2,1)}) %reduce-scatter.2.cloned.1.call-update) | async-done | bytes 1572880 | tf_op jit(solution)/shard_map/reduce_scatter | solution.py:48
  565.8 1.5 slice.36
  567.3 0.3 copy.23
  567.6 3.1 collective-permute-start
  570.7 0.1 copy.28
  570.8 0.1 copy.27
  570.9 0.1 copy.26
  571.0 0.5 collective-permute-done
  571.5 0.4 copy.24
  572.0 2.6 multiply_add_fusion
  574.6 1.6 copy-done.2
  576.2 0.9 fusion.37
  577.1 5.8 all-to-all-start
  582.9 0.0 all-gather.5.cloned.1.call-start
  582.9 117.7 %fusion.12 = f32[128,512,512]{2,1,0:T(8,128)} fusion(f32[128,16]{1,0:T(8,128)S(1)} %copy.28, f32[512]{0:T(512)S(1)} %iota_convert_fusion, f32[128,16]{1,0:T(8,128)S(1)} %copy.27, f32[128,16]{1,0:T(8,128)S(1)} %copy.26), kind=kOutput, calls=%fused_computation.15 | convolution fusion | flops 6445596672 | bytes 134244352 | tf_op jit(solution)/shard_map/cnt,cns->cts/dot_general | solution.py:22
  700.7 0.2 broadcast_compare_fusion
  700.9 0.0 all-to-all-done
  701.0 0.3 copy.25
  701.3 0.3 reshape_reshape.4
  701.6 2.8 fusion.34
  704.4 0.1 copy.29
  704.4 0.2 while.13
  704.6 0.1 copy.30
  704.8 71.1 %fusion = f32[128,4,512]{2,1,0:T(4,128)S(1)} fusion(f32[128,512,512]{2,1,0:T(8,128)} %fusion.12, pred[512,512]{1,0:T(8,128)(4,1)S(1)} %broadcast_compare_fusion, bf16[128,4,512]{2,1,0:T(4,128)(2,1)S(1)} %reshape_reshape.4), kind=kOutput, calls=%fused_computation.2 | convolution fusion | flops 1644167168 | bytes 136052736 | tf_op jit(solution)/shard_map/cts,bcs->bct/dot_general | solution.py:29
  775.9 2.9 fusion.31
  778.9 0.4 convert_element_type.101
  779.2 0.8 copy.31
  780.0 0.5 broadcast.38
  780.5 11.8 %reduce = bf16[2048,128]{1,0:T(8,128)(2,1)S(1)} reduce(bf16[2048,1,128]{2,1,0:T(2,128)(2,1)S(1)} %bitcast.55, bf16[]{:T(256)} %broadcast.38), dimensions={1}, to_apply=%bitcast.43.reduce_sub_computation | reduce | bytes 1048578
  792.3 0.1 reshape.83
  792.4 0.0 copy-start.5
  792.4 18.4 %all_to_all.24 = bf16[8,2,16384]{2,1,0:T(2,128)(2,1)S(1)} all-to-all(bf16[8,2,16384]{2,1,0:T(2,128)(2,1)S(1)} %reshape.83), channel_id=1, replica_groups=mesh['ctx'=8,'ch'=4] {'ctx'}, dimensions={0} | all-to-all | bytes 1048576 | tf_op jit(solution)/shard_map/all_to_all | solution.py:72
  810.9 0.5 reshape.84
  811.4 0.1 copy.32
  811.5 0.1 convert_bitcast_fusion
  811.6 0.3 copy.33
  811.9 2.9 fusion.39
  814.8 0.0 all-gather.5.cloned.1.call-update
  814.8 22.8 %all-gather.5.cloned.1.call-done = bf16[4096,256]{1,0:T(8,128)(2,1)} async-done(((bf16[1024,256]{1,0:T(8,128)(2,1)}), bf16[4096,256]{1,0:T(8,128)(2,1)}) %all-gather.5.cloned.1.call-update) | async-done | bytes 2097168 | tf_op jit(solution)/shard_map/all_gather | solution.py:84
  837.6 7.2 convolution_convert_fusion.1
  (27 shorter events, 0.2 us)
Async XLA Ops:
  6.5 487.4 %copy-start = (bf16[256,1024]{1,0:T(8,128)(2,1)S(1)}, bf16[256,1024]{1,0:T(8,128)(2,1)}, u32[]{:S(2)}) copy-start(bf16[256,1024]{1,0:T(8,128)(2,1)} %param.9) | copy-start | bytes 1572868
  6.5 487.4 %all-gather.3.cloned.1.call-start = ((), (), s32[]{:S(2)}) async-start(), calls=%async_computation.3 | async-start | bytes 28311552 | tf_op jit(solution)/shard_map/all_gather | solution.py:45
  11.3 554.5 %reduce-scatter.2.cloned.1.call-start = ((), (), s32[]{:S(2)}) async-start(), calls=%async_computation.4 | async-start | bytes 7864320 | tf_op jit(solution)/shard_map/reduce_scatter | solution.py:48
  507.3 1.5 copy-start.4
  565.8 6.2 copy-start.3
  567.6 3.9 collective-permute-start
  574.6 1.6 copy-start.2
  577.1 123.8 %all-to-all-start = ((bf16[8,128,256]{2,1,0:T(8,128)(2,1)}), bf16[8,128,256]{2,1,0:T(8,128)(2,1)S(1)}, u32[]{:S(2)}, u32[]{:S(2)}) async-start(bf16[8,128,256]{2,1,0:T(8,128)(2,1)} %bitcast.3), calls=%async_computation.1 | async-start | bytes 1048576 | tf_op jit(solution)/shard_map/all_to_all | solution.py:64
  582.9 254.7 %all-gather.5.cloned.1.call-start = ((), (), s32[]{:S(2)}) async-start(), calls=%async_computation.5 | async-start | bytes 2621440 | tf_op jit(solution)/shard_map/all_gather | solution.py:84
  792.4 19.5 %copy-start.5 = (f32[1024]{0:T(1024)S(1)}, f32[1024]{0:T(1024)}, u32[]{:S(2)}) copy-start(f32[1024]{0:T(1024)} %param.14) | copy-start | bytes 12292
  837.6 7.2 copy-start.1
Sparse Core Ops, SparseCore 0:
  11.4 482.5 all-gather.2
  507.4 58.3 reduce-scatter.1
  814.9 22.6 all-gather.4
where the time goes:
time: 857 us; the launch traced here: 852 us
  waiting for transfers between devices  563 us (66%)
  matrix products  215 us (25%)
  other arithmetic  20 us (2%)
  blocking collectives  18.4 us (2%)
  between operations  13.8 us (2%)
  local copies, waits for them, and re-layouts  12.5 us (1%)
  starting transfers between devices  8.92 us (1%)
    all_gather x1, waiting for transfers between devices, local(): lax.all_gather(in_weight, 'ctx', axis=2, tiled=True)  483 us
    dot_general x1, matrix products, local_conv(): toeplitz = jnp.einsum('cnt,cns->cts', falling, rising, precision=HIGHEST)  118 us
    dot_general x1, matrix products, local_conv(): within = jnp.einsum('cts,bcs->bct', toeplitz, pieces, precision=HIGHEST)  71.1 us
    reduce_scatter x1, waiting for transfers between devices, local(): lax.psum_scatter(terms.astype(jnp.bfloat16), 'ch', scatter_dimension=0, t...  57 us
    all_gather x1, waiting for transfers between devices, local(): lax.all_gather(gated, 'ch', axis=0, tiled=True)  22.8 us
    all_to_all x1, blocking collectives, local(): lax.all_to_all(full_out.reshape(1, chans, length).astype(jnp.bfloat16), '...  18.4 us
  transfers between devices with their start and end apart: 5, of which 4 were waited for; matrix products, arithmetic and copies ran while one was open for 14% of the time, Pallas kernels for 0%

commit v1 on v0

v1 whole, which is shorter than its diff:
```python
import functools

import jax
import jax.numpy as jnp
from jax import lax
from jax.experimental import pallas as pl
from jax.experimental.pallas import tpu as pltpu
from jax.sharding import PartitionSpec as P

LANES = 8


def conv_kernel(x_ref, taps_ref, decay_ref, gain_ref, skip_ref, out_ref, xs, ps, qs):
    _, length, chans = x_ref.shape
    modes = decay_ref.shape[0]
    reach = taps_ref.shape[1] - 1
    run = length // LANES
    rows = 256 if length % 256 == 0 else length

    def widen(k, _):
        at = pl.ds(pl.multiple_of(k * rows, rows), rows)
        for s in range(3):
            xs[s, at, :] = x_ref[s, at, :].astype(jnp.float32)
        return 0

    lax.fori_loop(0, length // rows, widen, 0)

    def wide(row):
        return jnp.broadcast_to(row, (LANES, chans))

    first = lax.broadcasted_iota(jnp.int32, (LANES, chans), 0) == 0
    rates = [decay_ref[n : n + 1, :] for n in range(modes)]
    a = [wide(jnp.exp(-r)) for r in rates]
    taps = [[wide(taps_ref[s, j : j + 1, :]) for j in range(reach + 1)] for s in range(3)]
    zero = jnp.zeros((LANES, chans), jnp.float32)

    def column(ref, t):
        return ref[pl.ds(t, LANES, stride=run), :]

    before = []
    for s in range(3):
        for j in range(1, reach + 1):
            last = column(xs.at[s], run - j)
            before.append(jnp.where(first, 0.0, pltpu.roll(last, 1, 0)))

    def sweep(t, carry):
        past, states = carry
        feats, now = [], []
        for s in range(3):
            x = column(xs.at[s], t)
            mine = past[s * reach : (s + 1) * reach]
            f = taps[s][0] * x
            for j in range(reach):
                f = f + taps[s][j + 1] * mine[j]
            feats.append(f)
            now += [x] + list(mine[: reach - 1])
        p = (feats[1] * feats[2]).astype(jnp.bfloat16).astype(jnp.float32)
        qs[pl.ds(t, LANES, stride=run), :] = feats[0]
        ps[pl.ds(t, LANES, stride=run), :] = p
        return tuple(now), tuple(a[n] * states[n] + p for n in range(modes))

    _, ends = lax.fori_loop(0, run, sweep, (tuple(before), (zero,) * modes), unroll=2)

    starts = []
    for n in range(modes):
        through = wide(jnp.exp(-rates[n] * float(run)))
        state = zero
        for _ in range(LANES - 1):
            state = jnp.where(first, 0.0, pltpu.roll(through * state + ends[n], 1, 0))
        starts.append(state)

    gain = [wide(gain_ref[n : n + 1, :]) for n in range(modes)]
    skip = wide(skip_ref[...])

    def emit(t, states):
        p = column(ps, t)
        states = tuple(a[n] * states[n] + p for n in range(modes))
        terms = [gain[n] * states[n] for n in range(modes)] + [skip * p]
        while len(terms) > 1:
            terms = [sum(terms[k : k + 2][1:], terms[k]) for k in range(0, len(terms), 2)]
        at = pl.ds(t, LANES, stride=run)
        qs[at, :] = qs[at, :] * terms[0]
        return states

    lax.fori_loop(0, run, emit, tuple(starts), unroll=2)

    def narrow(k, _):
        at = pl.ds(pl.multiple_of(k * rows, rows), rows)
        out_ref[at, :] = qs[at, :].astype(jnp.bfloat16)
        return 0

    lax.fori_loop(0, length // rows, narrow, 0)


def convolve(projected, taps, decay, gain, skip):
    _, length, chans = projected.shape
    return pl.pallas_call(
        conv_kernel,
        out_shape=jax.ShapeDtypeStruct((length, chans), jnp.bfloat16),
        in_specs=[pl.BlockSpec(memory_space=pltpu.VMEM)] * 5,
        out_specs=pl.BlockSpec(memory_space=pltpu.VMEM),
        scratch_shapes=[
            pltpu.VMEM((3, length, chans), jnp.float32),
            pltpu.VMEM((length, chans), jnp.float32),
            pltpu.VMEM((length, chans), jnp.float32),
        ],
        compiler_params=pltpu.CompilerParams(vmem_limit_bytes=60 << 20),
    )(projected, taps, decay, gain, skip)


def own_parameters(short_filter, decay_rates, residues, skip_gain, chans):
    n_ctx, n_ch = lax.axis_size("ctx"), lax.axis_size("ch")
    start = lax.axis_index("ctx") * chans
    flat = short_filter.reshape(short_filter.shape[0], -1)
    packed = jnp.concatenate([flat, decay_rates, residues, skip_gain[:, None]], axis=1)
    piece = lax.dynamic_slice_in_dim(packed, start, chans, 0)
    pairs = []
    for s in range(n_ctx):
        for c in range(n_ch):
            pairs.append((s * n_ch + c, c * n_ctx + s))
    mine = lax.ppermute(piece, ("ctx", "ch"), pairs).T
    n_taps, order = flat.shape[1], decay_rates.shape[1]
    taps = mine[:n_taps].reshape(short_filter.shape[1], short_filter.shape[2], chans)
    decay = mine[n_taps : n_taps + order]
    gain = mine[n_taps + order : n_taps + 2 * order] * jnp.sqrt(-jnp.expm1(-2.0 * decay))
    return taps, decay, gain, mine[n_taps + 2 * order :]


def local(tokens, in_weight, short_filter, decay_rates, residues, skip_gain, out_weight):
    n_ctx, n_ch = lax.axis_size("ctx"), lax.axis_size("ch")
    rows_here = tokens.shape[0]
    chans = in_weight.shape[2] // n_ch
    taps, decay, gain, skip = own_parameters(short_filter, decay_rates, residues, skip_gain, chans)
    everyone = lax.all_gather(tokens, "ctx", axis=0, tiled=True)
    terms = jnp.einsum("rd,dsc->src", everyone, in_weight, preferred_element_type=jnp.float32)
    projected = lax.psum_scatter(terms.astype(jnp.bfloat16), "ch", scatter_dimension=2, tiled=True)
    gated = convolve(projected, taps, decay, gain, skip)
    sent = gated.reshape(n_ctx, rows_here, chans)
    mine = lax.all_to_all(sent, "ctx", split_axis=0, concat_axis=0, tiled=True)
    every = lax.all_gather(mine, "ch", axis=0)
    weight = out_weight.reshape(n_ctx, n_ch, chans, out_weight.shape[1])
    mixed = jnp.einsum("jirc,ijcd->rd", every, weight, preferred_element_type=jnp.float32)
    return mixed.astype(jnp.bfloat16)


def solution(mesh):
    in_specs = (
        P("ctx", "ch"),
        P("ch", None, "ctx"),
        P("ch", None, None),
        P("ch", None),
        P("ch", None),
        P("ch"),
        P(None, "ch"),
    )
    out_specs = P("ctx", "ch")
    return jax.shard_map(local, mesh=mesh, in_specs=in_specs, out_specs=out_specs, check_vma=False)
```

time: 857 us -> 255 us (0.30)
  waiting for transfers between devices: 563 us -> 151 us
  matrix products: 215 us -> 18 us
  local copies, waits for them, and re-layouts: 12.5 us -> 36.7 us
  other arithmetic: 20 us -> 0.7 us
  Pallas kernels: 0 us -> 12.1 us
    all_gather x2, waiting for transfers between devices: 505 us -> 98.9 us  [the longest x1 76.5 us: local(): everyone = lax.all_gather(tokens, 'ctx', axis=0, tiled=True)]
    dot_general x6 -> x2, matrix products: 215 us -> 18 us  [the longest x1 10.9 us: local(): jnp.einsum('rd,dsc->src', everyone, in_weight, preferred_element_type=jnp...]
    reduce_scatter x1 -> x0, waiting for transfers between devices: 57 us -> none  [local(): lax.psum_scatter(terms.astype(jnp.bfloat16), 'ch', scatter_dimension=0, t...]
    unnamed x3 -> x4, waiting for transfers between devices: 0.05 us -> 50.6 us
    unnamed x19 -> x14, local copies, waits for them, and re-layouts: 7.66 us -> 35.5 us
    pallas_call x0 -> x1, Pallas kernels: none -> 12.1 us  [convolve(): pl.pallas_call(conv_kernel, out_shape=jax.ShapeDtypeStruct((length, chans...]
    unnamed x2 -> x0, other arithmetic: 11.8 us -> none
  transfers between devices with their start and end apart: 5 -> 4, of which waited for: 4 -> 4; matrix products, arithmetic and copies ran while one was open for 14% -> 1% of each run, Pallas kernels for 0% -> 0%
where the time goes in v1:
time: 255 us
  waiting for transfers between devices  151 us (59%)
  local copies, waits for them, and re-layouts  36.7 us (14%)
  blocking collectives  19 us (7%)
  matrix products  18 us (7%)
  between operations  13.1 us (5%)
  Pallas kernels  12.1 us (5%)
  starting transfers between devices  4.28 us (2%)
    all_gather x1, waiting for transfers between devices, local(): everyone = lax.all_gather(tokens, 'ctx', axis=0, tiled=True)  76.5 us
    unnamed x4, waiting for transfers between devices  50.6 us
    unnamed x14, local copies, waits for them, and re-layouts  35.5 us
    all_gather x1, waiting for transfers between devices, local(): every = lax.all_gather(mine, 'ch', axis=0)  22.4 us
    all_to_all x1, blocking collectives, local(): mine = lax.all_to_all(sent, 'ctx', split_axis=0, concat_axis=0, tiled=True)  19 us
    pallas_call x1, Pallas kernels, convolve(): pl.pallas_call(conv_kernel, out_shape=jax.ShapeDtypeStruct((length, chans...  12.1 us
    dot_general x1, matrix products, local(): jnp.einsum('rd,dsc->src', everyone, in_weight, preferred_element_type=jnp...  10.9 us
    dot_general x1, matrix products, local(): jnp.einsum('jirc,ijcd->rd', every, weight, preferred_element_type=jnp.flo...  7.14 us
  transfers between devices with their start and end apart: 4, of which 4 were waited for; matrix products, arithmetic and copies ran while one was open for 1% of the time, Pallas kernels for 0%

profile of v1, /device:TPU:1, one launch (start us, length us, event | category | flops | bytes accessed | tf_op | source)
XLA Modules:
  0.0 254.6 jit_solution(11304844238456946351)
XLA Ops:
  6.5 0.0 copy-start
  6.5 0.0 all-gather.4.cloned.1.call-start
  6.5 0.7 all-gather.4.cloned.1.call-update
  7.3 0.0 reduce-scatter.4.cloned.1.call-start
  7.3 76.5 %all-gather.4.cloned.1.call-done = bf16[2048,1024]{1,0:T(8,128)(2,1)} async-done(((bf16[256,1024]{1,0:T(8,128)(2,1)}), bf16[2048,1024]{1,0:T(8,128)(2,1)}) %all-gather.4.cloned.1.call-update) | async-done | bytes 4194320 | tf_op jit(solution)/shard_map/all_gather | solution.py:134
  83.8 0.0 copy-done
  83.8 10.9 %convert_bitcast_fusion = bf16[3,2048,512]{1,2,0:T(8,128)(2,1)} fusion(bf16[1024,3,512]{2,0,1:T(8,128)(2,1)S(1)} %copy-done, bf16[2048,1024]{1,0:T(8,128)(2,1)} %all-gather.4.cloned.1.call-done), kind=kOutput, calls=%fused_computation | convolution fusion | flops 6445596672 | bytes 13631488 | tf_op jit(solution)/shard_map/rd,dsc->src/dot_general | solution.py:135
  94.7 11.4 %copy.18 = bf16[3,2048,512]{1,0,2:T(4,128)(2,1)} copy(bf16[3,2048,512]{1,2,0:T(8,128)(2,1)} %convert_bitcast_fusion) | data formatting | bytes 12582912
  106.1 13.5 %copy.21 = bf16[64,8,3,2048]{3,1,2,0:T(8,128)(2,1)} copy(bf16[64,8,3,2048]{3,2,1,0:T(4,128)(2,1)} %bitcast.24) | data formatting | bytes 12582912
  119.6 0.0 copy-start.3
  119.6 0.0 copy-start.1
  119.6 0.0 copy-start.2
  119.6 0.0 copy-start.4
  119.6 0.0 reduce-scatter.4.cloned.1.call-update
  119.6 0.0 all-gather.6.cloned.1.call-start
  119.7 0.7 copy-done.3
  120.4 0.0 copy-done.1
  120.5 0.0 copy-done.2
  120.5 0.0 copy-done.4
  120.5 0.1 fusion.11
  120.6 4.2 %collective-permute-start = (f32[128,42]{0,1:T(8,128)S(1)}, f32[128,42]{0,1:T(8,128)S(1)}, u32[]{:S(2)}, u32[]{:S(2)}) collective-permute-start(f32[128,42]{0,1:T(8,128)S(1)} %fusion.11), channel_id=1, source_target_pairs={{0,0},{1,8},{2,16},{3,24},{4,1},{5,9},{6,17},{7,25},{8,2},{9,10},{... | collective-permute-start | bytes 64520 | tf_op jit(solution)/shard_map/ppermute | solution.py:121
  124.8 1.2 collective-permute-done
  126.0 0.5 slice.19.skip_ref
  126.5 0.6 reshape.13.taps_ref
  127.1 0.6 slice_multiply_fusion
  127.7 49.8 %reduce-scatter.4.cloned.1.call-done = bf16[128,6144]{1,0:T(8,128)(2,1)} async-done(((bf16[512,6144]{1,0:T(8,128)(2,1)}), bf16[128,6144]{1,0:T(8,128)(2,1)}) %reduce-scatter.4.cloned.1.call-update) | async-done | bytes 1572880
  177.6 5.6 %reshape.20 = bf16[128,3,2048]{2,1,0:T(4,128)(2,1)} reshape(bf16[128,6144]{1,0:T(8,128)(2,1)} %reduce-scatter.4.cloned.1.call-done) | data formatting | bytes 3145728
  183.2 4.3 %copy.19.x_ref = bf16[3,2048,128]{2,1,0:T(8,128)(2,1)} copy(bf16[3,2048,128]{1,0,2:T(4,128)(2,1)} %bitcast.26) | data formatting | bytes 3145728
  187.4 12.1 %shard_map.73 = bf16[2048,128]{1,0:T(8,128)(2,1)} custom-call(bf16[3,2048,128]{2,1,0:T(8,128)(2,1)} %copy.19.x_ref, f32[3,3,128]{2,1,0:T(4,128)} %reshape.13.taps_ref, f32[16,128]{1,0:T(8,128)} %get-tuple-element.6.decay_ref, f32[16,128]{1,0:T(8,128)} %get-tuple-element.5.gain_ref, f32[1,128]{1,0:T(1,128)} %slice.19.skip_ref), custom_call_target="tpu_custom_call" | custom-call | tf_op jit(solution)/shard_map/pallas_call | solution.py:97
  199.6 19.0 %all_to_all.5 = bf16[8,256,128]{2,1,0:T(8,128)(2,1)} all-to-all(bf16[8,256,128]{2,1,0:T(8,128)(2,1)} %bitcast.27), channel_id=1, replica_groups=mesh['ctx'=8,'ch'=4] {'ctx'}, dimensions={0} | all-to-all | bytes 1048576 | tf_op jit(solution)/shard_map/all_to_all | solution.py:139
  218.6 0.0 all-gather.6.cloned.1.call-update
  218.6 22.4 %all-gather.6.cloned.1.call-done = bf16[32,256,128]{2,1,0:T(8,128)(2,1)} async-done(((bf16[8,256,128]{2,1,0:T(8,128)(2,1)}), bf16[32,256,128]{2,1,0:T(8,128)(2,1)}) %all-gather.6.cloned.1.call-update) | async-done | bytes 2097168 | tf_op jit(solution)/shard_map/all_gather | solution.py:140
  240.9 7.1 %fusion.6 = bf16[256,1024]{1,0:T(8,128)(2,1)} fusion(bf16[8,4,128,1024]{3,2,1,0:T(8,128)(2,1)} %bitcast.32, bf16[4,8,256,128]{3,2,1,0:T(8,128)(2,1)} %bitcast.33), kind=kOutput, calls=%fused_computation.5 | convolution fusion | flops 2147745792 | bytes 11010048 | tf_op jit(solution)/shard_map/jirc,ijcd->rd/dot_general | solution.py:142
  (2 shorter events, 0.0 us)
Async XLA Ops:
  6.5 77.3 %copy-start = (bf16[1024,3,512]{2,0,1:T(8,128)(2,1)S(1)}, bf16[1024,3,512]{2,0,1:T(8,128)(2,1)}, u32[]{:S(2)}) copy-start(bf16[1024,3,512]{2,0,1:T(8,128)(2,1)} %param.8) | copy-start | bytes 9437188
  6.5 77.3 %all-gather.4.cloned.1.call-start = ((), (), s32[]{:S(2)}) async-start(), calls=%async_computation.2 | async-start | bytes 4718592 | tf_op jit(solution)/shard_map/all_gather | solution.py:134
  7.3 170.3 %reduce-scatter.4.cloned.1.call-start = ((), (), s32[]{:S(2)}) async-start(), calls=%async_computation.4 | async-start | bytes 7864320
  119.6 0.8 copy-start.3
  119.6 0.9 copy-start.1
  119.6 0.9 copy-start.2
  119.6 0.9 copy-start.4
  119.6 121.3 %all-gather.6.cloned.1.call-start = ((), (), s32[]{:S(2)}) async-start(), calls=%async_computation.3 | async-start | bytes 2621440 | tf_op jit(solution)/shard_map/all_gather | solution.py:140
  120.6 5.4 %collective-permute-start = (f32[128,42]{0,1:T(8,128)S(1)}, f32[128,42]{0,1:T(8,128)S(1)}, u32[]{:S(2)}, u32[]{:S(2)}) collective-permute-start(f32[128,42]{0,1:T(8,128)S(1)} %fusion.11), channel_id=1, source_target_pairs={{0,0},{1,8},{2,16},{3,24},{4,1},{5,9},{6,17},{7,25},{8,2},{9,10},{... | collective-permute-start | bytes 64520 | tf_op jit(solution)/shard_map/ppermute | solution.py:121
Sparse Core Ops, SparseCore 0:
  9.5 74.2 all-gather.3
  119.7 57.8 reduce-scatter.3
  218.7 22.1 all-gather.5

commit v2 on v1

--- a/solution.py
+++ b/solution.py
@@ -106,6 +106,342 @@
         ],
         compiler_params=pltpu.CompilerParams(vmem_limit_bytes=60 << 20),
     )(projected, taps, decay, gain, skip)
+
+
+MESH = pl.DeviceIdType.MESH
+
+
+def remote(src, dst, send, recv, device):
+    return pltpu.make_async_remote_copy(
+        src_ref=src, dst_ref=dst, send_sem=send, recv_sem=recv, device_id=device, device_id_type=MESH
+    )
+
+
+def project_kernel(
+    n_ctx, tok_ref, w_hbm, out_ref, held, w, part, near, sums, far,
+    w_sem, up_s, down_s, line_r, pair_s, pair_r, near_s, near_r, far_s, far_r,
+):
+    rows = tok_ref.shape[0]
+    streams, _, width = w.shape
+    chans = width // 4
+    line = n_ctx // 2
+    ctx, ch = lax.axis_index("ctx"), lax.axis_index("ch")
+    z, x = lax.div(ctx, 2), lax.rem(ctx, 2)
+    y, core = lax.div(ch, 2), lax.rem(ch, 2)
+    near_ch, far_ch = y * 2 + 1 - core, (1 - y) * 2 + core
+    has_up, has_down = z + 1 < line, z > 0
+
+    load = pltpu.make_async_copy(w_hbm, w, w_sem)
+    load.start()
+    held[ctx] = tok_ref[...]
+
+    barrier = pltpu.get_barrier_semaphore()
+
+    def greet(*device):
+        pl.semaphore_signal(barrier, inc=1, device_id=device, device_id_type=MESH)
+
+    greet(z * 2 + 1 - x, ch)
+    greet(ctx, near_ch)
+    greet(ctx, far_ch)
+
+    @pl.when(has_up)
+    def _():
+        greet(ctx + 2, ch)
+
+    @pl.when(has_down)
+    def _():
+        greet(ctx - 2, ch)
+
+    pl.semaphore_wait(barrier, 3 + has_up.astype(jnp.int32) + has_down.astype(jnp.int32))
+
+    def up_copy(src):
+        at = held.at[src * 2 + x]
+        return remote(at, at, up_s.at[src], line_r.at[src], (ctx + 2, ch))
+
+    def down_copy(src):
+        at = held.at[src * 2 + x]
+        return remote(at, at, down_s.at[src], line_r.at[src], (ctx - 2, ch))
+
+    def pair_copy(src, side):
+        at = held.at[src * 2 + side]
+        return remote(at, at, pair_s.at[src], pair_r.at[src], (z * 2 + 1 - x, ch))
+
+    def near_copy(r):
+        return remote(part.at[1 - core, r], near.at[r], near_s.at[r], near_r.at[r], (ctx, near_ch))
+
+    def far_copy(r):
+        return remote(sums.at[r], far.at[r], far_s.at[r], far_r.at[r], (ctx, far_ch))
+
+    @pl.when(has_up)
+    def _():
+        up_copy(z).start()
+
+    @pl.when(has_down)
+    def _():
+        down_copy(z).start()
+
+    pair_copy(z, x).start()
+    load.wait()
+
+    def compute(r):
+        def stream(s, _):
+            for half in range(2):
+                acc = jnp.dot(
+                    held[r],
+                    w[s, :, half * 2 * chans : (half + 1) * 2 * chans],
+                    preferred_element_type=jnp.float32,
+                ).astype(jnp.bfloat16)
+                part[0, r, half, s] = acc[:, :chans]
+                part[1, r, half, s] = acc[:, chans:]
+            return 0
+
+        lax.fori_loop(0, streams, stream, 0)
+        near_copy(r).start()
+
+    def combine(r):
+        near_copy(r).wait_recv()
+        for s in range(streams):
+            both = part[core, r, 1 - y, s].astype(jnp.float32) + near[r, 1 - y, s].astype(jnp.float32)
+            sums[r, s] = both.astype(jnp.bfloat16)
+        far_copy(r).start()
+
+    def place(s):
+        away = lax.div(s + 1, 2)
+        sign = 2 * lax.rem(s + 1, 2) - 1
+        at = z + away * sign
+        return at, sign, (s >= 0) & (at >= 0) & (at < line)
+
+    def step(s, _):
+        at, sign, valid = place(s)
+
+        @pl.when(valid)
+        def _():
+            @pl.when(s > 0)
+            def _():
+                up_copy(at).wait_recv()
+
+                @pl.when((sign < 0) & has_up)
+                def _():
+                    up_copy(at).start()
+
+                @pl.when((sign > 0) & has_down)
+                def _():
+                    down_copy(at).start()
+
+                pair_copy(at, x).start()
+
+            compute(at * 2 + x)
+
+        at1, _, valid1 = place(s - 1)
+
+        @pl.when(valid1)
+        def _():
+            pair_copy(at1, 1 - x).wait_recv()
+            compute(at1 * 2 + 1 - x)
+            combine(at1 * 2 + x)
+
+        at2, _, valid2 = place(s - 2)
+
+        @pl.when(valid2)
+        def _():
+            combine(at2 * 2 + 1 - x)
+
+        return 0
+
+    lax.fori_loop(0, 2 * line + 1, step, 0)
+
+    def finish(r, _):
+        far_copy(r).wait_recv()
+        at = pl.ds(pl.multiple_of(r * rows, rows), rows)
+        for s in range(streams):
+            total = part[core, r, y, s].astype(jnp.float32) + near[r, y, s].astype(jnp.float32)
+            out_ref[s, at, :] = (total + far[r, s].astype(jnp.float32)).astype(jnp.bfloat16)
+        return 0
+
+    lax.fori_loop(0, n_ctx, finish, 0)
+
+    def drain(r, _):
+        near_copy(r).wait_send()
+        far_copy(r).wait_send()
+        return 0
+
+    lax.fori_loop(0, n_ctx, drain, 0)
+
+    def drain_line(src, _):
+        pair_copy(src, x).wait_send()
+
+        @pl.when(has_up & (src <= z))
+        def _():
+            up_copy(src).wait_send()
+
+        @pl.when(has_down & (src >= z))
+        def _():
+            down_copy(src).wait_send()
+
+        return 0
+
+    lax.fori_loop(0, line, drain_line, 0)
+
+
+def project(tokens, in_weight):
+    n_ctx = lax.axis_size("ctx")
+    rows, depth = tokens.shape
+    streams, width = in_weight.shape[1:]
+    chans = width // 4
+    dma = pltpu.SemaphoreType.DMA
+    line = n_ctx // 2
+    return pl.pallas_call(
+        functools.partial(project_kernel, n_ctx),
+        out_shape=jax.ShapeDtypeStruct((streams, n_ctx * rows, chans), jnp.bfloat16),
+        in_specs=[pl.BlockSpec(memory_space=pltpu.VMEM), pl.BlockSpec(memory_space=pl.ANY)],
+        out_specs=pl.BlockSpec(memory_space=pltpu.VMEM),
+        scratch_shapes=[
+            pltpu.VMEM((n_ctx, rows, depth), jnp.bfloat16),
+            pltpu.VMEM((streams, depth, width), jnp.bfloat16),
+            pltpu.VMEM((2, n_ctx, 2, streams, rows, chans), jnp.bfloat16),
+            pltpu.VMEM((n_ctx, 2, streams, rows, chans), jnp.bfloat16),
+            pltpu.VMEM((n_ctx, streams, rows, chans), jnp.bfloat16),
+            pltpu.VMEM((n_ctx, streams, rows, chans), jnp.bfloat16),
+            dma,
+        ]
+        + [dma((line,))] * 5
+        + [dma((n_ctx,))] * 4,
+        compiler_params=pltpu.CompilerParams(
+            collective_id=0, has_side_effects=True, vmem_limit_bytes=48 << 20
+        ),
+    )(tokens, jnp.transpose(in_weight, (1, 0, 2)))
+
+
+def mix_kernel(
+    n_ctx, g_ref, w_hbm, out_ref, blocks, w, acc,
+    w_sem, sent_s, sent_r, far_s, far_r, near_s, near_r, relay_s, relay_r,
+):
+    chans = g_ref.shape[2]
+    width = 4 * chans
+    ctx, ch = lax.axis_index("ctx"), lax.axis_index("ch")
+    y, core = lax.div(ch, 2), lax.rem(ch, 2)
+    near_ch, far_ch, cross_ch = y * 2 + 1 - core, (1 - y) * 2 + core, (1 - y) * 2 + 1 - core
+    load = pltpu.make_async_copy(w_hbm, w, w_sem)
+    load.start()
+
+    def lanes(j):
+        return pl.ds(pl.multiple_of(j * chans, chans), chans)
+
+    def peer(k):
+        return lax.rem(ctx + k, n_ctx)
+
+    barrier = pltpu.get_barrier_semaphore()
+
+    def greet(device):
+        pl.semaphore_signal(barrier, inc=1, device_id=device, device_id_type=MESH)
+
+    def greet_peer(k, _):
+        greet((peer(k), ch))
+        return 0
+
+    lax.fori_loop(1, n_ctx, greet_peer, 0)
+    greet((ctx, near_ch))
+    greet((ctx, far_ch))
+    blocks[ctx, :, lanes(ch)] = g_ref[ctx]
+    acc[...] = jnp.zeros_like(acc)
+    pl.semaphore_wait(barrier, n_ctx + 1)
+
+    def sent_copy(dest):
+        return remote(
+            g_ref.at[dest], blocks.at[ctx, :, lanes(ch)], sent_s.at[dest], sent_r.at[ctx], (dest, ch)
+        )
+
+    def arrival(src):
+        at = blocks.at[src, :, lanes(ch)]
+        return remote(at, at, sent_s.at[src], sent_r.at[src], (src, ch))
+
+    def far_copy(src, j):
+        at = blocks.at[src, :, lanes(j)]
+        return remote(at, at, far_s.at[src], far_r.at[src], (ctx, far_ch))
+
+    def near_copy(src, j):
+        at = blocks.at[src, :, lanes(j)]
+        return remote(at, at, near_s.at[src], near_r.at[src], (ctx, near_ch))
+
+    def relay_copy(src, j):
+        at = blocks.at[src, :, lanes(j)]
+        return remote(at, at, relay_s.at[src], relay_r.at[src], (ctx, near_ch))
+
+    def send(k, _):
+        sent_copy(peer(k)).start()
+        return 0
+
+    lax.fori_loop(1, n_ctx, send, 0)
+
+    def step(k, _):
+        @pl.when(k < n_ctx)
+        def _():
+            src = peer(n_ctx - k)
+
+            @pl.when(k > 0)
+            def _():
+                arrival(src).wait_recv()
+
+            far_copy(src, ch).start()
+            near_copy(src, ch).start()
+
+        @pl.when((k >= 1) & (k <= n_ctx))
+        def _():
+            src = peer(n_ctx - k + 1)
+            far_copy(src, far_ch).wait_recv()
+            relay_copy(src, far_ch).start()
+
+        @pl.when(k == 1)
+        def _():
+            load.wait()
+
+        @pl.when(k >= 2)
+        def _():
+            src = peer(n_ctx - k + 2)
+            near_copy(src, near_ch).wait_recv()
+            relay_copy(src, cross_ch).wait_recv()
+            at = pl.ds(pl.multiple_of(src * width, width), width)
+            acc[...] += jnp.dot(blocks[src], w[at, :], preferred_element_type=jnp.float32)
+
+        return 0
+
+    lax.fori_loop(0, n_ctx + 2, step, 0)
+    out_ref[...] = acc[...].astype(jnp.bfloat16)
+
+    def drain(k, _):
+        src = peer(k)
+
+        @pl.when(k > 0)
+        def _():
+            sent_copy(src).wait_send()
+
+        far_copy(src, ch).wait_send()
+        near_copy(src, ch).wait_send()
+        relay_copy(src, far_ch).wait_send()
+        return 0
+
+    lax.fori_loop(0, n_ctx, drain, 0)
+
+
+def mix(gated, out_weight):
+    n_ctx, rows, chans = gated.shape
+    dma = pltpu.SemaphoreType.DMA
+    return pl.pallas_call(
+        functools.partial(mix_kernel, n_ctx),
+        out_shape=jax.ShapeDtypeStruct((rows, out_weight.shape[1]), jnp.bfloat16),
+        in_specs=[pl.BlockSpec(memory_space=pltpu.VMEM), pl.BlockSpec(memory_space=pl.ANY)],
+        out_specs=pl.BlockSpec(memory_space=pltpu.VMEM),
+        scratch_shapes=[
+            pltpu.VMEM((n_ctx, rows, 4 * chans), jnp.bfloat16),
+            pltpu.VMEM(out_weight.shape, jnp.bfloat16),
+            pltpu.VMEM((rows, out_weight.shape[1]), jnp.float32),
+            dma,
+        ]
+        + [dma((n_ctx,))] * 8,
+        compiler_params=pltpu.CompilerParams(
+            collective_id=1, has_side_effects=True, vmem_limit_bytes=48 << 20
+        ),
+    )(gated, out_weight)
 
 
 def own_parameters(short_filter, decay_rates, residues, skip_gain, chans):
@@ -131,6 +467,9 @@
     rows_here = tokens.shape[0]
     chans = in_weight.shape[2] // n_ch
     taps, decay, gain, skip = own_parameters(short_filter, decay_rates, residues, skip_gain, chans)
+    if n_ch == 4 and n_ctx % 2 == 0 and chans % 128 == 0:
+        gated = convolve(project(tokens, in_weight), taps, decay, gain, skip)
+        return mix(gated.reshape(n_ctx, rows_here, chans), out_weight)
     everyone = lax.all_gather(tokens, "ctx", axis=0, tiled=True)
     terms = jnp.einsum("rd,dsc->src", everyone, in_weight, preferred_element_type=jnp.float32)
     projected = lax.psum_scatter(terms.astype(jnp.bfloat16), "ch", scatter_dimension=2, tiled=True)

time: 255 us -> 131 us (0.51)
  waiting for transfers between devices: 151 us -> 0.01 us
  Pallas kernels: 12.1 us -> 116 us
  local copies, waits for them, and re-layouts: 36.7 us -> 7.91 us
  blocking collectives: 19 us -> 0 us
  matrix products: 18 us -> 0 us
  between operations: 13.1 us -> 0.05 us
    pallas_call x0 -> x2, Pallas kernels: none -> 104 us  [the longest x1 76.8 us: project(): pl.pallas_call(functools.partial(project_kernel, n_ctx), out_shape=jax.Sh...]
    all_gather x2 -> x0, waiting for transfers between devices: 98.9 us -> none  [the longest x1 76.5 us: local(): everyone = lax.all_gather(tokens, 'ctx', axis=0, tiled=True)]
    unnamed x4 -> x0, waiting for transfers between devices: 50.6 us -> none
    unnamed x14 -> x9, local copies, waits for them, and re-layouts: 35.5 us -> 5.91 us
    all_to_all x1 -> x0, blocking collectives: 19 us -> none  [local(): mine = lax.all_to_all(sent, 'ctx', split_axis=0, concat_axis=0, tiled=True)]
    dot_general x2 -> x0, matrix products: 18 us -> none  [the longest x1 10.9 us: local(): jnp.einsum('rd,dsc->src', everyone, in_weight, preferred_element_type=jnp...]
  transfers between devices with their start and end apart: 4 -> 1, of which waited for: 4 -> 0; matrix products, arithmetic and copies ran while one was open for 1% -> 0% of each run, Pallas kernels for 0% -> 59%
where the time goes in v2:
time: 131 us; the launch traced here: 130 us
  Pallas kernels  116 us (89%)
  local copies, waits for them, and re-layouts  7.91 us (6%)
  starting transfers between devices  4.58 us (3%)
  other arithmetic  1.43 us (1%)
    pallas_call x1, Pallas kernels, project(): pl.pallas_call(functools.partial(project_kernel, n_ctx), out_shape=jax.Sh...  76.8 us
    pallas_call x1, Pallas kernels, mix(): pl.pallas_call(functools.partial(mix_kernel, n_ctx), out_shape=jax.ShapeD...  27.1 us
    pallas_call x1, Pallas kernels, convolve(): pl.pallas_call(conv_kernel, out_shape=jax.ShapeDtypeStruct((length, chans...  12.1 us
    unnamed x9, local copies, waits for them, and re-layouts  5.91 us
    ppermute x1, starting transfers between devices, own_parameters(): mine = lax.ppermute(piece, ('ctx', 'ch'), pairs).T  4.58 us
  transfers between devices with their start and end apart: 1, of which 0 were waited for; matrix products, arithmetic and copies ran while one was open for 0% of the time, Pallas kernels for 59%

profile of v2, /device:TPU:1, one launch (start us, length us, event | category | flops | bytes accessed | tf_op | source)
XLA Modules:
  0.0 130.0 jit_solution(8155112637503495277)
XLA Ops:
  0.0 0.8 reshape.9
  0.8 0.8 fusion.2
  1.6 4.6 %collective-permute-start = (f32[128,42]{0,1:T(8,128)S(1)}, f32[128,42]{0,1:T(8,128)S(1)}, u32[]{:S(2)}, u32[]{:S(2)}) collective-permute-start(f32[128,42]{0,1:T(8,128)S(1)} %fusion.2), channel_id=1, source_target_pairs={{0,0},{1,8},{2,16},{3,24},{4,1},{5,9},{6,17},{7,25},{8,2},{9,10},{... | collective-permute-start | bytes 64520 | tf_op jit(solution)/shard_map/ppermute | solution.py:457
  6.2 0.0 copy-start.1
  6.2 1.9 %copy-done.1 = bf16[1024,3,512]{2,0,1:T(8,128)(2,1)S(1)} copy-done((bf16[1024,3,512]{2,0,1:T(8,128)(2,1)S(1)}, bf16[1024,3,512]{2,0,1:T(8,128)(2,1)}, u32[]{:S(2)}) %copy-start.1) | copy-done | bytes 3145752
  8.1 0.0 copy-start.3
  8.1 1.0 copy-done.3
  9.1 76.8 %shard_map.73.x_ref = bf16[3,2048,128]{2,1,0:T(8,128)(2,1)S(1)} custom-call(bf16[256,1024]{1,0:T(8,128)(2,1)S(1)} %copy-done.3, bf16[3,1024,512]{2,1,0:T(8,128)(2,1)S(1)} %bitcast.6), custom_call_target="tpu_custom_call" | custom-call | tf_op jit(solution)/shard_map/pallas_call | solution.py:293
  85.9 0.0 copy-start
  86.0 1.1 copy-done
  87.1 0.0 collective-permute-done
  87.1 0.6 slice.19.skip_ref
  87.7 0.6 slice_multiply_fusion
  88.3 0.6 reshape.10.taps_ref
  88.9 12.1 %shard_map.74 = bf16[2048,128]{1,0:T(8,128)(2,1)} custom-call(bf16[3,2048,128]{2,1,0:T(8,128)(2,1)} %copy-done, f32[3,3,128]{2,1,0:T(4,128)} %reshape.10.taps_ref, f32[16,128]{1,0:T(8,128)} %get-tuple-element.6.decay_ref, f32[16,128]{1,0:T(8,128)} %get-tuple-element.5.gain_ref, f32[1,128]{1,0:T(1,128)} %slice.19.skip_ref), custom_call_target="tpu_custom_call" | custom-call | tf_op jit(solution)/shard_map/pallas_call | solution.py:97
  101.1 0.0 copy-start.2
  101.1 1.0 copy-done.2
  102.1 27.1 %shard_map.75 = bf16[256,1024]{1,0:T(8,128)(2,1)S(1)} custom-call(bf16[8,256,128]{2,1,0:T(8,128)(2,1)S(1)} %bitcast.7, bf16[4096,1024]{1,0:T(8,128)(2,1)} %w_hbm.1), custom_call_target="tpu_custom_call" | custom-call | tf_op jit(solution)/shard_map/pallas_call | solution.py:429
  129.2 0.8 copy.9
  (1 shorter events, 0.0 us)
Async XLA Ops:
  1.6 85.5 %collective-permute-start = (f32[128,42]{0,1:T(8,128)S(1)}, f32[128,42]{0,1:T(8,128)S(1)}, u32[]{:S(2)}, u32[]{:S(2)}) collective-permute-start(f32[128,42]{0,1:T(8,128)S(1)} %fusion.2), channel_id=1, source_target_pairs={{0,0},{1,8},{2,16},{3,24},{4,1},{5,9},{6,17},{7,25},{8,2},{9,10},{... | collective-permute-start | bytes 64520 | tf_op jit(solution)/shard_map/ppermute | solution.py:457
  6.2 1.9 %copy-start.1 = (bf16[1024,3,512]{2,0,1:T(8,128)(2,1)S(1)}, bf16[1024,3,512]{2,0,1:T(8,128)(2,1)}, u32[]{:S(2)}) copy-start(bf16[1024,3,512]{2,0,1:T(8,128)(2,1)} %param.8) | copy-start | bytes 9437188
  8.1 1.0 copy-start.3
  85.9 1.2 copy-start
  101.1 1.0 copy-start.2

commit v3 on v2

--- a/solution.py
+++ b/solution.py
@@ -118,10 +118,10 @@
 
 
 def project_kernel(
-    n_ctx, tok_ref, w_hbm, out_ref, held, w, part, near, sums, far,
-    w_sem, up_s, down_s, line_r, pair_s, pair_r, near_s, near_r, far_s, far_r,
+    n_ctx, cuts, tok_ref, w_hbm, out_ref, held, w, part, near, sums, far,
+    w_sem, tok_sem, up_s, down_s, line_r, pair_s, pair_r, near_s, near_r, far_s, far_r,
 ):
-    rows = tok_ref.shape[0]
+    rows = held.shape[1]
     streams, _, width = w.shape
     chans = width // 4
     line = n_ctx // 2
@@ -133,7 +133,13 @@
 
     load = pltpu.make_async_copy(w_hbm, w, w_sem)
     load.start()
-    held[ctx] = tok_ref[...]
+    own = []
+    for q in range(cuts):
+        fetch = pltpu.make_async_copy(
+            tok_ref.at[pl.ds(q * rows, rows), :], held.at[ctx * cuts + q], tok_sem.at[q]
+        )
+        fetch.start()
+        own.append(fetch)
 
     barrier = pltpu.get_barrier_semaphore()
 
@@ -154,16 +160,19 @@
 
     pl.semaphore_wait(barrier, 3 + has_up.astype(jnp.int32) + has_down.astype(jnp.int32))
 
+    def slot(src, side):
+        return (lax.div(src, cuts) * 2 + side) * cuts + lax.rem(src, cuts)
+
     def up_copy(src):
-        at = held.at[src * 2 + x]
+        at = held.at[slot(src, x)]
         return remote(at, at, up_s.at[src], line_r.at[src], (ctx + 2, ch))
 
     def down_copy(src):
-        at = held.at[src * 2 + x]
+        at = held.at[slot(src, x)]
         return remote(at, at, down_s.at[src], line_r.at[src], (ctx - 2, ch))
 
     def pair_copy(src, side):
-        at = held.at[src * 2 + side]
+        at = held.at[slot(src, side)]
         return remote(at, at, pair_s.at[src], pair_r.at[src], (z * 2 + 1 - x, ch))
 
     def near_copy(r):
@@ -172,15 +181,19 @@
     def far_copy(r):
         return remote(sums.at[r], far.at[r], far_s.at[r], far_r.at[r], (ctx, far_ch))
 
-    @pl.when(has_up)
-    def _():
-        up_copy(z).start()
-
-    @pl.when(has_down)
-    def _():
-        down_copy(z).start()
-
-    pair_copy(z, x).start()
+    for q in range(cuts):
+        own[q].wait()
+
+        @pl.when(has_up)
+        def _():
+            up_copy(z * cuts + q).start()
+
+        @pl.when(has_down)
+        def _():
+            down_copy(z * cuts + q).start()
+
+        pair_copy(z * cuts + q, x).start()
+
     load.wait()
 
     def compute(r):
@@ -205,18 +218,19 @@
             sums[r, s] = both.astype(jnp.bfloat16)
         far_copy(r).start()
 
-    def place(s):
+    def place(t):
+        s = lax.div(t + cuts, cuts) - 1
         away = lax.div(s + 1, 2)
         sign = 2 * lax.rem(s + 1, 2) - 1
         at = z + away * sign
-        return at, sign, (s >= 0) & (at >= 0) & (at < line)
+        return at * cuts + lax.rem(t + cuts, cuts), sign, (t >= 0) & (at >= 0) & (at < line)
 
     def step(s, _):
         at, sign, valid = place(s)
 
         @pl.when(valid)
         def _():
-            @pl.when(s > 0)
+            @pl.when(s >= cuts)
             def _():
                 up_copy(at).wait_recv()
 
@@ -230,25 +244,25 @@
 
                 pair_copy(at, x).start()
 
-            compute(at * 2 + x)
+            compute(slot(at, x))
 
         at1, _, valid1 = place(s - 1)
 
         @pl.when(valid1)
         def _():
             pair_copy(at1, 1 - x).wait_recv()
-            compute(at1 * 2 + 1 - x)
-            combine(at1 * 2 + x)
+            compute(slot(at1, 1 - x))
+            combine(slot(at1, x))
 
         at2, _, valid2 = place(s - 2)
 
         @pl.when(valid2)
         def _():
-            combine(at2 * 2 + 1 - x)
-
-        return 0
-
-    lax.fori_loop(0, 2 * line + 1, step, 0)
+            combine(slot(at2, 1 - x))
+
+        return 0
+
+    lax.fori_loop(0, (2 * line - 1) * cuts + 2, step, 0)
 
     def finish(r, _):
         far_copy(r).wait_recv()
@@ -258,56 +272,59 @@
             out_ref[s, at, :] = (total + far[r, s].astype(jnp.float32)).astype(jnp.bfloat16)
         return 0
 
-    lax.fori_loop(0, n_ctx, finish, 0)
+    lax.fori_loop(0, n_ctx * cuts, finish, 0)
 
     def drain(r, _):
         near_copy(r).wait_send()
         far_copy(r).wait_send()
         return 0
 
-    lax.fori_loop(0, n_ctx, drain, 0)
+    lax.fori_loop(0, n_ctx * cuts, drain, 0)
 
     def drain_line(src, _):
         pair_copy(src, x).wait_send()
 
-        @pl.when(has_up & (src <= z))
+        @pl.when(has_up & (lax.div(src, cuts) <= z))
         def _():
             up_copy(src).wait_send()
 
-        @pl.when(has_down & (src >= z))
+        @pl.when(has_down & (lax.div(src, cuts) >= z))
         def _():
             down_copy(src).wait_send()
 
         return 0
 
-    lax.fori_loop(0, line, drain_line, 0)
+    lax.fori_loop(0, line * cuts, drain_line, 0)
 
 
 def project(tokens, in_weight):
     n_ctx = lax.axis_size("ctx")
-    rows, depth = tokens.shape
+    cuts = 2
+    rows, depth = tokens.shape[0] // cuts, tokens.shape[1]
+    slots = n_ctx * cuts
     streams, width = in_weight.shape[1:]
     chans = width // 4
     dma = pltpu.SemaphoreType.DMA
     line = n_ctx // 2
     return pl.pallas_call(
-        functools.partial(project_kernel, n_ctx),
-        out_shape=jax.ShapeDtypeStruct((streams, n_ctx * rows, chans), jnp.bfloat16),
-        in_specs=[pl.BlockSpec(memory_space=pltpu.VMEM), pl.BlockSpec(memory_space=pl.ANY)],
+        functools.partial(project_kernel, n_ctx, cuts),
+        out_shape=jax.ShapeDtypeStruct((streams, slots * rows, chans), jnp.bfloat16),
+        in_specs=[pl.BlockSpec(memory_space=pl.ANY)] * 2,
         out_specs=pl.BlockSpec(memory_space=pltpu.VMEM),
         scratch_shapes=[
-            pltpu.VMEM((n_ctx, rows, depth), jnp.bfloat16),
+            pltpu.VMEM((slots, rows, depth), jnp.bfloat16),
             pltpu.VMEM((streams, depth, width), jnp.bfloat16),
-            pltpu.VMEM((2, n_ctx, 2, streams, rows, chans), jnp.bfloat16),
-            pltpu.VMEM((n_ctx, 2, streams, rows, chans), jnp.bfloat16),
-            pltpu.VMEM((n_ctx, streams, rows, chans), jnp.bfloat16),
-            pltpu.VMEM((n_ctx, streams, rows, chans), jnp.bfloat16),
+            pltpu.VMEM((2, slots, 2, streams, rows, chans), jnp.bfloat16),
+            pltpu.VMEM((slots, 2, streams, rows, chans), jnp.bfloat16),
+            pltpu.VMEM((slots, streams, rows, chans), jnp.bfloat16),
+            pltpu.VMEM((slots, streams, rows, chans), jnp.bfloat16),
             dma,
+            dma((cuts,)),
         ]
-        + [dma((line,))] * 5
-        + [dma((n_ctx,))] * 4,
+        + [dma((line * cuts,))] * 5
+        + [dma((slots,))] * 4,
         compiler_params=pltpu.CompilerParams(
-            collective_id=0, has_side_effects=True, vmem_limit_bytes=48 << 20
+            collective_id=0, has_side_effects=True, vmem_limit_bytes=62 << 20
         ),
     )(tokens, jnp.transpose(in_weight, (1, 0, 2)))
 
@@ -439,7 +456,7 @@
         ]
         + [dma((n_ctx,))] * 8,
         compiler_params=pltpu.CompilerParams(
-            collective_id=1, has_side_effects=True, vmem_limit_bytes=48 << 20
+            collective_id=1, has_side_effects=True, vmem_limit_bytes=62 << 20
         ),
     )(gated, out_weight)
 

time: 131 us -> 124 us (0.947)
  local copies, waits for them, and re-layouts: 7.91 us -> 3.88 us
  Pallas kernels: 116 us -> 114 us
    unnamed x9 -> x1, local copies, waits for them, and re-layouts: 5.91 us -> 1.87 us
    pallas_call x1, Pallas kernels: 76.8 us -> 74 us  [project(): pl.pallas_call(functools.partial(project_kernel, n_ctx, cuts), out_shape=...]
  transfers between devices with their start and end apart: 1 -> 1, of which waited for: 0 -> 0; matrix products, arithmetic and copies ran while one was open for 0% -> 0% of each run, Pallas kernels for 59% -> 60%
where the time goes in v3:
time: 124 us
  Pallas kernels  114 us (92%)
  starting transfers between devices  4.58 us (4%)
  local copies, waits for them, and re-layouts  3.88 us (3%)
  other arithmetic  1.43 us (1%)
    pallas_call x1, Pallas kernels, project(): pl.pallas_call(functools.partial(project_kernel, n_ctx, cuts), out_shape=...  74 us
    pallas_call x1, Pallas kernels, mix(): pl.pallas_call(functools.partial(mix_kernel, n_ctx), out_shape=jax.ShapeD...  27.5 us
    pallas_call x1, Pallas kernels, convolve(): pl.pallas_call(conv_kernel, out_shape=jax.ShapeDtypeStruct((length, chans...  12.1 us
    ppermute x1, starting transfers between devices, own_parameters(): mine = lax.ppermute(piece, ('ctx', 'ch'), pairs).T  4.58 us
  transfers between devices with their start and end apart: 1, of which 0 were waited for; matrix products, arithmetic and copies ran while one was open for 0% of the time, Pallas kernels for 60%

profile of v3, /device:TPU:1, one launch (start us, length us, event | category | flops | bytes accessed | tf_op | source)
XLA Modules:
  0.0 123.6 jit_solution(11584308359283209552)
XLA Ops:
  0.0 0.8 reshape.9
  0.8 0.8 fusion.2
  1.6 4.6 %collective-permute-start = (f32[128,42]{0,1:T(8,128)S(1)}, f32[128,42]{0,1:T(8,128)S(1)}, u32[]{:S(2)}, u32[]{:S(2)}) collective-permute-start(f32[128,42]{0,1:T(8,128)S(1)} %fusion.2), channel_id=1, source_target_pairs={{0,0},{1,8},{2,16},{3,24},{4,1},{5,9},{6,17},{7,25},{8,2},{9,10},{... | collective-permute-start | bytes 64520 | tf_op jit(solution)/shard_map/ppermute | solution.py:474
  6.2 74.0 %shard_map.73.x_ref = bf16[3,2048,128]{2,1,0:T(8,128)(2,1)} custom-call(bf16[256,1024]{1,0:T(8,128)(2,1)} %tok_ref.1, bf16[3,1024,512]{2,1,0:T(8,128)(2,1)} %bitcast.6), custom_call_target="tpu_custom_call" | custom-call | tf_op jit(solution)/shard_map/pallas_call | solution.py:309
  80.2 0.0 collective-permute-done
  80.3 0.6 slice.19.skip_ref
  80.8 0.6 slice_multiply_fusion
  81.5 0.6 reshape.10.taps_ref
  82.1 12.1 %shard_map.74 = bf16[2048,128]{1,0:T(8,128)(2,1)} custom-call(bf16[3,2048,128]{2,1,0:T(8,128)(2,1)} %shard_map.73.x_ref, f32[3,3,128]{2,1,0:T(4,128)} %reshape.10.taps_ref, f32[16,128]{1,0:T(8,128)} %get-tuple-element.6.decay_ref, f32[16,128]{1,0:T(8,128)} %get-tuple-element.5.gain_ref, f32[1,128]{1,0:T(1,128)} %slice.19.skip_ref), custom_call_target="tpu_custom_call" | custom-call | tf_op jit(solution)/shard_map/pallas_call | solution.py:97
  94.2 27.5 %shard_map.75 = bf16[256,1024]{1,0:T(8,128)(2,1)} custom-call(bf16[8,256,128]{2,1,0:T(8,128)(2,1)} %bitcast.7, bf16[4096,1024]{1,0:T(8,128)(2,1)} %w_hbm.1), custom_call_target="tpu_custom_call" | custom-call | tf_op jit(solution)/shard_map/pallas_call | solution.py:446
  121.8 1.9 %copy.9 = bf16[256,1024]{1,0:T(8,128)(2,1)} copy(bf16[256,1024]{1,0:T(8,128)(2,1)} %shard_map.75) | data formatting | bytes 1048576
  (1 shorter events, 0.0 us)
Async XLA Ops:
  1.6 78.6 %collective-permute-start = (f32[128,42]{0,1:T(8,128)S(1)}, f32[128,42]{0,1:T(8,128)S(1)}, u32[]{:S(2)}, u32[]{:S(2)}) collective-permute-start(f32[128,42]{0,1:T(8,128)S(1)} %fusion.2), channel_id=1, source_target_pairs={{0,0},{1,8},{2,16},{3,24},{4,1},{5,9},{6,17},{7,25},{8,2},{9,10},{... | collective-permute-start | bytes 64520 | tf_op jit(solution)/shard_map/ppermute | solution.py:474

commit v4 on v3

--- a/solution.py
+++ b/solution.py
@@ -330,10 +330,14 @@
 
 
 def mix_kernel(
-    n_ctx, g_ref, w_hbm, out_ref, blocks, w, acc,
+    n_ctx, x_ref, taps_ref, decay_ref, gain_ref, skip_ref, w_hbm, out_ref,
+    g_ref, xs, ps, qs, entering, blocks, w, acc,
     w_sem, sent_s, sent_r, far_s, far_r, near_s, near_r, relay_s, relay_r,
 ):
-    chans = g_ref.shape[2]
+    _, rows, chans = g_ref.shape
+    modes = decay_ref.shape[0]
+    reach = taps_ref.shape[1] - 1
+    run = rows // LANES
     width = 4 * chans
     ctx, ch = lax.axis_index("ctx"), lax.axis_index("ch")
     y, core = lax.div(ch, 2), lax.rem(ch, 2)
@@ -359,9 +363,81 @@
     lax.fori_loop(1, n_ctx, greet_peer, 0)
     greet((ctx, near_ch))
     greet((ctx, far_ch))
-    blocks[ctx, :, lanes(ch)] = g_ref[ctx]
     acc[...] = jnp.zeros_like(acc)
+
+    def wide(row):
+        return jnp.broadcast_to(row, (LANES, chans))
+
+    sub = lax.broadcasted_iota(jnp.int32, (LANES, chans), 0)
+    zero = jnp.zeros((LANES, chans), jnp.float32)
+    rates = [decay_ref[n : n + 1, :] for n in range(modes)]
+    a = [wide(jnp.exp(-r)) for r in rates]
+    taps = [[wide(taps_ref[s, j : j + 1, :]) for j in range(reach + 1)] for s in range(3)]
+    for s in range(3):
+        xs[s, 0:8, :] = jnp.zeros((8, chans), jnp.float32)
+
+    def absorb(k, carry):
+        base = pl.multiple_of(k * rows, rows)
+        for s in range(3):
+            xs[s, pl.ds(base + 8, rows), :] = x_ref[s, pl.ds(base, rows), :].astype(jnp.float32)
+        before = []
+        for s in range(3):
+            for j in range(1, reach + 1):
+                before.append(xs[s, pl.ds(base + 8 - j, LANES, stride=run), :])
+
+        def sweep(t, inner):
+            past, states = inner
+            feats, now = [], []
+            for s in range(3):
+                x = xs[s, pl.ds(base + 8 + t, LANES, stride=run), :]
+                mine = past[s * reach : (s + 1) * reach]
+                f = taps[s][0] * x
+                for j in range(reach):
+                    f = f + taps[s][j + 1] * mine[j]
+                feats.append(f)
+                now += [x] + list(mine[: reach - 1])
+            p = (feats[1] * feats[2]).astype(jnp.bfloat16).astype(jnp.float32)
+            qs[pl.ds(base + t, LANES, stride=run), :] = feats[0]
+            ps[pl.ds(base + t, LANES, stride=run), :] = p
+            return tuple(now), tuple(a[n] * states[n] + p for n in range(modes))
+
+        _, ends = lax.fori_loop(0, run, sweep, (tuple(before), (zero,) * modes), unroll=2)
+        following = []
+        for n in range(modes):
+            through = wide(jnp.exp(-rates[n] * float(run)))
+            state = jnp.where(sub == 0, carry[n], pltpu.roll(ends[n], 1, 0))
+            power, by = through, 1
+            while by < LANES:
+                state = state + jnp.where(sub >= by, power * pltpu.roll(state, by, 0), 0.0)
+                power, by = power * power, by * 2
+            entering[k, n] = state
+            following.append(pltpu.roll(through * state + ends[n], 1, 0))
+        return tuple(following)
+
+    lax.fori_loop(0, n_ctx, absorb, (zero,) * modes)
     pl.semaphore_wait(barrier, n_ctx + 1)
+    gain = [wide(gain_ref[n : n + 1, :]) for n in range(modes)]
+    skip = wide(skip_ref[...])
+
+    def emit_block(k):
+        base = pl.multiple_of(k * rows, rows)
+
+        def emit(t, states):
+            at = pl.ds(base + t, LANES, stride=run)
+            p = ps[at, :]
+            states = tuple(a[n] * states[n] + p for n in range(modes))
+            terms = [gain[n] * states[n] for n in range(modes)] + [skip * p]
+            while len(terms) > 1:
+                terms = [sum(terms[i : i + 2][1:], terms[i]) for i in range(0, len(terms), 2)]
+            qs[at, :] = qs[at, :] * terms[0]
+            return states
+
+        lax.fori_loop(0, run, emit, tuple(entering[k, n] for n in range(modes)), unroll=2)
+        g_ref[k] = qs[pl.ds(base, rows), :].astype(jnp.bfloat16)
+
+    def offset(k):
+        odd = lax.rem(k, 2)
+        return n_ctx // 2 + (1 - odd) * lax.div(k, 2) - odd * lax.div(k + 1, 2)
 
     def sent_copy(dest):
         return remote(
@@ -385,15 +461,26 @@
         return remote(at, at, relay_s.at[src], relay_r.at[src], (ctx, near_ch))
 
     def send(k, _):
-        sent_copy(peer(k)).start()
-        return 0
-
-    lax.fori_loop(1, n_ctx, send, 0)
+        dest = peer(offset(k))
+        emit_block(dest)
+
+        @pl.when(k < n_ctx - 1)
+        def _():
+            sent_copy(dest).start()
+
+        return 0
+
+    lax.fori_loop(0, n_ctx, send, 0)
+    blocks[ctx, :, lanes(ch)] = g_ref[ctx]
+
+    def source(k):
+        own = jnp.where(k == 0, 0, n_ctx - offset(k - 1))
+        return lax.rem(ctx + own, n_ctx)
 
     def step(k, _):
         @pl.when(k < n_ctx)
         def _():
-            src = peer(n_ctx - k)
+            src = source(k)
 
             @pl.when(k > 0)
             def _():
@@ -404,7 +491,7 @@
 
         @pl.when((k >= 1) & (k <= n_ctx))
         def _():
-            src = peer(n_ctx - k + 1)
+            src = source(k - 1)
             far_copy(src, far_ch).wait_recv()
             relay_copy(src, far_ch).start()
 
@@ -414,7 +501,7 @@
 
         @pl.when(k >= 2)
         def _():
-            src = peer(n_ctx - k + 2)
+            src = source(k - 2)
             near_copy(src, near_ch).wait_recv()
             relay_copy(src, cross_ch).wait_recv()
             at = pl.ds(pl.multiple_of(src * width, width), width)
@@ -440,15 +527,22 @@
     lax.fori_loop(0, n_ctx, drain, 0)
 
 
-def mix(gated, out_weight):
-    n_ctx, rows, chans = gated.shape
+def mix(projected, taps, decay, gain, skip, out_weight):
+    n_ctx = lax.axis_size("ctx")
+    streams, length, chans = projected.shape
+    rows = length // n_ctx
     dma = pltpu.SemaphoreType.DMA
     return pl.pallas_call(
         functools.partial(mix_kernel, n_ctx),
         out_shape=jax.ShapeDtypeStruct((rows, out_weight.shape[1]), jnp.bfloat16),
-        in_specs=[pl.BlockSpec(memory_space=pltpu.VMEM), pl.BlockSpec(memory_space=pl.ANY)],
+        in_specs=[pl.BlockSpec(memory_space=pltpu.VMEM)] * 5 + [pl.BlockSpec(memory_space=pl.ANY)],
         out_specs=pl.BlockSpec(memory_space=pltpu.VMEM),
         scratch_shapes=[
+            pltpu.VMEM((n_ctx, rows, chans), jnp.bfloat16),
+            pltpu.VMEM((streams, length + 8, chans), jnp.float32),
+            pltpu.VMEM((length, chans), jnp.float32),
+            pltpu.VMEM((length, chans), jnp.float32),
+            pltpu.VMEM((n_ctx, decay.shape[0], LANES, chans), jnp.float32),
             pltpu.VMEM((n_ctx, rows, 4 * chans), jnp.bfloat16),
             pltpu.VMEM(out_weight.shape, jnp.bfloat16),
             pltpu.VMEM((rows, out_weight.shape[1]), jnp.float32),
@@ -458,7 +552,7 @@
         compiler_params=pltpu.CompilerParams(
             collective_id=1, has_side_effects=True, vmem_limit_bytes=62 << 20
         ),
-    )(gated, out_weight)
+    )(projected, taps, decay, gain, skip, out_weight)
 
 
 def own_parameters(short_filter, decay_rates, residues, skip_gain, chans):
@@ -484,9 +578,8 @@
     rows_here = tokens.shape[0]
     chans = in_weight.shape[2] // n_ch
     taps, decay, gain, skip = own_parameters(short_filter, decay_rates, residues, skip_gain, chans)
-    if n_ch == 4 and n_ctx % 2 == 0 and chans % 128 == 0:
-        gated = convolve(project(tokens, in_weight), taps, decay, gain, skip)
-        return mix(gated.reshape(n_ctx, rows_here, chans), out_weight)
+    if n_ch == 4 and n_ctx % 2 == 0 and chans % 128 == 0 and rows_here % 64 == 0:
+        return mix(project(tokens, in_weight), taps, decay, gain, skip, out_weight)
     everyone = lax.all_gather(tokens, "ctx", axis=0, tiled=True)
     terms = jnp.einsum("rd,dsc->src", everyone, in_weight, preferred_element_type=jnp.float32)
     projected = lax.psum_scatter(terms.astype(jnp.bfloat16), "ch", scatter_dimension=2, tiled=True)

time: 124 us -> 116 us (0.935)
  Pallas kernels: 114 us -> 106 us
    pallas_call x1 -> x0, Pallas kernels: 12.1 us -> none  [convolve(): pl.pallas_call(conv_kernel, out_shape=jax.ShapeDtypeStruct((length, chans...]
    pallas_call x1, Pallas kernels: 27.5 us -> 32 us  [mix(): pl.pallas_call(functools.partial(mix_kernel, n_ctx), out_shape=jax.ShapeD...]
  transfers between devices with their start and end apart: 1 -> 1, of which waited for: 0 -> 0; matrix products, arithmetic and copies ran while one was open for 0% -> 0% of each run, Pallas kernels for 60% -> 64%
where the time goes in v4:
time: 116 us
  Pallas kernels  106 us (91%)
  starting transfers between devices  4.58 us (4%)
  local copies, waits for them, and re-layouts  3.85 us (3%)
  other arithmetic  1.43 us (1%)
    pallas_call x1, Pallas kernels, project(): pl.pallas_call(functools.partial(project_kernel, n_ctx, cuts), out_shape=...  74 us
    pallas_call x1, Pallas kernels, mix(): pl.pallas_call(functools.partial(mix_kernel, n_ctx), out_shape=jax.ShapeD...  32 us
    ppermute x1, starting transfers between devices, own_parameters(): mine = lax.ppermute(piece, ('ctx', 'ch'), pairs).T  4.58 us
  transfers between devices with their start and end apart: 1, of which 0 were waited for; matrix products, arithmetic and copies ran while one was open for 0% of the time, Pallas kernels for 64%

profile of v4, /device:TPU:1, one launch (start us, length us, event | category | flops | bytes accessed | tf_op | source)
XLA Modules:
  0.0 116.0 jit_solution(3281051474467784440)
XLA Ops:
  0.0 0.8 reshape.6
  0.8 0.8 fusion.2
  1.6 4.6 %collective-permute-start = (f32[128,42]{0,1:T(8,128)S(1)}, f32[128,42]{0,1:T(8,128)S(1)}, u32[]{:S(2)}, u32[]{:S(2)}) collective-permute-start(f32[128,42]{0,1:T(8,128)S(1)} %fusion.2), channel_id=1, source_target_pairs={{0,0},{1,8},{2,16},{3,24},{4,1},{5,9},{6,17},{7,25},{8,2},{9,10},{... | collective-permute-start | bytes 64520 | tf_op jit(solution)/shard_map/ppermute | solution.py:568
  6.2 74.0 %shard_map.73.x_ref = bf16[3,2048,128]{2,1,0:T(8,128)(2,1)} custom-call(bf16[256,1024]{1,0:T(8,128)(2,1)} %tok_ref.1, bf16[3,1024,512]{2,1,0:T(8,128)(2,1)} %bitcast.5), custom_call_target="tpu_custom_call" | custom-call | tf_op jit(solution)/shard_map/pallas_call | solution.py:309
  80.2 0.0 collective-permute-done
  80.3 0.6 slice.19.skip_ref
  80.8 0.6 slice_multiply_fusion
  81.4 0.6 reshape.7.taps_ref
  82.0 32.0 %shard_map.74 = bf16[256,1024]{1,0:T(8,128)(2,1)} custom-call(bf16[3,2048,128]{2,1,0:T(8,128)(2,1)} %shard_map.73.x_ref, f32[3,3,128]{2,1,0:T(4,128)} %reshape.7.taps_ref, f32[16,128]{1,0:T(8,128)} %get-tuple-element.6.decay_ref, f32[16,128]{1,0:T(8,128)} %get-tuple-element.5.gain_ref, f32[1,128]{1,0:T(1,128)} %slice.19.skip_ref, bf16[4096,1024]{1,0:T(8,128)(2,1)} %w_hbm.1), custom_call_target="tpu_custom_call" | custom-call | tf_op jit(solution)/shard_map/pallas_call | solution.py:535
  114.1 1.9 %copy.9 = bf16[256,1024]{1,0:T(8,128)(2,1)} copy(bf16[256,1024]{1,0:T(8,128)(2,1)} %shard_map.74) | data formatting | bytes 1048576
  (1 shorter events, 0.0 us)
Async XLA Ops:
  1.6 78.6 %collective-permute-start = (f32[128,42]{0,1:T(8,128)S(1)}, f32[128,42]{0,1:T(8,128)S(1)}, u32[]{:S(2)}, u32[]{:S(2)}) collective-permute-start(f32[128,42]{0,1:T(8,128)S(1)} %fusion.2), channel_id=1, source_target_pairs={{0,0},{1,8},{2,16},{3,24},{4,1},{5,9},{6,17},{7,25},{8,2},{9,10},{... | collective-permute-start | bytes 64520 | tf_op jit(solution)/shard_map/ppermute | solution.py:568

commit v5 on v4

--- a/solution.py
+++ b/solution.py
@@ -218,6 +218,8 @@
             sums[r, s] = both.astype(jnp.bfloat16)
         far_copy(r).start()
 
+    late = 2 * cuts - 1
+
     def place(t):
         s = lax.div(t + cuts, cuts) - 1
         away = lax.div(s + 1, 2)
@@ -246,15 +248,20 @@
 
             compute(slot(at, x))
 
-        at1, _, valid1 = place(s - 1)
+        at1, _, valid1 = place(s - late)
 
         @pl.when(valid1)
         def _():
             pair_copy(at1, 1 - x).wait_recv()
             compute(slot(at1, 1 - x))
-            combine(slot(at1, x))
-
-        at2, _, valid2 = place(s - 2)
+
+        at3, _, valid3 = place(s - 1)
+
+        @pl.when(valid3)
+        def _():
+            combine(slot(at3, x))
+
+        at2, _, valid2 = place(s - late - 1)
 
         @pl.when(valid2)
         def _():
@@ -262,7 +269,7 @@
 
         return 0
 
-    lax.fori_loop(0, (2 * line - 1) * cuts + 2, step, 0)
+    lax.fori_loop(0, (2 * line - 1) * cuts + late + 1, step, 0)
 
     def finish(r, _):
         far_copy(r).wait_recv()

time: 116 us -> 107 us (0.922)
  Pallas kernels: 106 us -> 96.5 us
    pallas_call x1, Pallas kernels: 74 us -> 64.4 us  [project(): pl.pallas_call(functools.partial(project_kernel, n_ctx, cuts), out_shape=...]
  transfers between devices with their start and end apart: 1 -> 1, of which waited for: 0 -> 0; matrix products, arithmetic and copies ran while one was open for 0% -> 0% of each run, Pallas kernels for 64% -> 61%
where the time goes in v5:
time: 107 us; the launch traced here: 106 us
  Pallas kernels  96.5 us (90%)
  starting transfers between devices  4.58 us (4%)
  local copies, waits for them, and re-layouts  3.85 us (4%)
  other arithmetic  1.43 us (1%)
    pallas_call x1, Pallas kernels, project(): pl.pallas_call(functools.partial(project_kernel, n_ctx, cuts), out_shape=...  64.4 us
    pallas_call x1, Pallas kernels, mix(): pl.pallas_call(functools.partial(mix_kernel, n_ctx), out_shape=jax.ShapeD...  32.1 us
    ppermute x1, starting transfers between devices, own_parameters(): mine = lax.ppermute(piece, ('ctx', 'ch'), pairs).T  4.58 us
  transfers between devices with their start and end apart: 1, of which 0 were waited for; matrix products, arithmetic and copies ran while one was open for 0% of the time, Pallas kernels for 61%

profile of v5, /device:TPU:1, one launch (start us, length us, event | category | flops | bytes accessed | tf_op | source)
XLA Modules:
  0.0 106.4 jit_solution(10275656988524872392)
XLA Ops:
  0.0 0.8 reshape.6
  0.8 0.8 fusion.2
  1.6 4.6 %collective-permute-start = (f32[128,42]{0,1:T(8,128)S(1)}, f32[128,42]{0,1:T(8,128)S(1)}, u32[]{:S(2)}, u32[]{:S(2)}) collective-permute-start(f32[128,42]{0,1:T(8,128)S(1)} %fusion.2), channel_id=1, source_target_pairs={{0,0},{1,8},{2,16},{3,24},{4,1},{5,9},{6,17},{7,25},{8,2},{9,10},{... | collective-permute-start | bytes 64520 | tf_op jit(solution)/shard_map/ppermute | solution.py:575
  6.2 64.4 %shard_map.73.x_ref = bf16[3,2048,128]{2,1,0:T(8,128)(2,1)} custom-call(bf16[256,1024]{1,0:T(8,128)(2,1)} %tok_ref.1, bf16[3,1024,512]{2,1,0:T(8,128)(2,1)} %bitcast.5), custom_call_target="tpu_custom_call" | custom-call | tf_op jit(solution)/shard_map/pallas_call | solution.py:316
  70.6 0.0 collective-permute-done
  70.7 0.6 slice.19.skip_ref
  71.2 0.6 slice_multiply_fusion
  71.8 0.6 reshape.7.taps_ref
  72.4 32.1 %shard_map.74 = bf16[256,1024]{1,0:T(8,128)(2,1)} custom-call(bf16[3,2048,128]{2,1,0:T(8,128)(2,1)} %shard_map.73.x_ref, f32[3,3,128]{2,1,0:T(4,128)} %reshape.7.taps_ref, f32[16,128]{1,0:T(8,128)} %get-tuple-element.6.decay_ref, f32[16,128]{1,0:T(8,128)} %get-tuple-element.5.gain_ref, f32[1,128]{1,0:T(1,128)} %slice.19.skip_ref, bf16[4096,1024]{1,0:T(8,128)(2,1)} %w_hbm.1), custom_call_target="tpu_custom_call" | custom-call | tf_op jit(solution)/shard_map/pallas_call | solution.py:542
  104.5 1.9 %copy.9 = bf16[256,1024]{1,0:T(8,128)(2,1)} copy(bf16[256,1024]{1,0:T(8,128)(2,1)} %shard_map.74) | data formatting | bytes 1048576
  (1 shorter events, 0.0 us)
Async XLA Ops:
  1.6 69.0 %collective-permute-start = (f32[128,42]{0,1:T(8,128)S(1)}, f32[128,42]{0,1:T(8,128)S(1)}, u32[]{:S(2)}, u32[]{:S(2)}) collective-permute-start(f32[128,42]{0,1:T(8,128)S(1)} %fusion.2), channel_id=1, source_target_pairs={{0,0},{1,8},{2,16},{3,24},{4,1},{5,9},{6,17},{7,25},{8,2},{9,10},{... | collective-permute-start | bytes 64520 | tf_op jit(solution)/shard_map/ppermute | solution.py:575

commit v6 on v5

--- a/solution.py
+++ b/solution.py
@@ -408,7 +408,7 @@
             ps[pl.ds(base + t, LANES, stride=run), :] = p
             return tuple(now), tuple(a[n] * states[n] + p for n in range(modes))
 
-        _, ends = lax.fori_loop(0, run, sweep, (tuple(before), (zero,) * modes), unroll=2)
+        _, ends = lax.fori_loop(0, run, sweep, (tuple(before), (zero,) * modes), unroll=4)
         following = []
         for n in range(modes):
             through = wide(jnp.exp(-rates[n] * float(run)))
@@ -439,7 +439,7 @@
             qs[at, :] = qs[at, :] * terms[0]
             return states
 
-        lax.fori_loop(0, run, emit, tuple(entering[k, n] for n in range(modes)), unroll=2)
+        lax.fori_loop(0, run, emit, tuple(entering[k, n] for n in range(modes)), unroll=4)
         g_ref[k] = qs[pl.ds(base, rows), :].astype(jnp.bfloat16)
 
     def offset(k):

time: 107 us -> 107 us (level)
  no operation moved by 1% of the time
where the time goes in v6:
time: 107 us; the launch traced here: 106 us
  Pallas kernels  96.4 us (90%)
  starting transfers between devices  4.58 us (4%)
  local copies, waits for them, and re-layouts  3.85 us (4%)
  other arithmetic  1.43 us (1%)
    pallas_call x1, Pallas kernels, project(): pl.pallas_call(functools.partial(project_kernel, n_ctx, cuts), out_shape=...  64.4 us
    pallas_call x1, Pallas kernels, mix(): pl.pallas_call(functools.partial(mix_kernel, n_ctx), out_shape=jax.ShapeD...  31.9 us
    ppermute x1, starting transfers between devices, own_parameters(): mine = lax.ppermute(piece, ('ctx', 'ch'), pairs).T  4.58 us
  transfers between devices with their start and end apart: 1, of which 0 were waited for; matrix products, arithmetic and copies ran while one was open for 0% of the time, Pallas kernels for 61%

profile of v6, /device:TPU:1, one launch (start us, length us, event | category | flops | bytes accessed | tf_op | source)
XLA Modules:
  0.0 106.3 jit_solution(17960440935119806534)
XLA Ops:
  0.0 0.8 reshape.6
  0.8 0.8 fusion.2
  1.6 4.6 %collective-permute-start = (f32[128,42]{0,1:T(8,128)S(1)}, f32[128,42]{0,1:T(8,128)S(1)}, u32[]{:S(2)}, u32[]{:S(2)}) collective-permute-start(f32[128,42]{0,1:T(8,128)S(1)} %fusion.2), channel_id=1, source_target_pairs={{0,0},{1,8},{2,16},{3,24},{4,1},{5,9},{6,17},{7,25},{8,2},{9,10},{... | collective-permute-start | bytes 64520 | tf_op jit(solution)/shard_map/ppermute | solution.py:575
  6.2 64.4 %shard_map.73.x_ref = bf16[3,2048,128]{2,1,0:T(8,128)(2,1)} custom-call(bf16[256,1024]{1,0:T(8,128)(2,1)} %tok_ref.1, bf16[3,1024,512]{2,1,0:T(8,128)(2,1)} %bitcast.5), custom_call_target="tpu_custom_call" | custom-call | tf_op jit(solution)/shard_map/pallas_call | solution.py:316
  70.6 0.0 collective-permute-done
  70.7 0.6 slice.19.skip_ref
  71.2 0.6 slice_multiply_fusion
  71.8 0.6 reshape.7.taps_ref
  72.4 31.9 %shard_map.74 = bf16[256,1024]{1,0:T(8,128)(2,1)} custom-call(bf16[3,2048,128]{2,1,0:T(8,128)(2,1)} %shard_map.73.x_ref, f32[3,3,128]{2,1,0:T(4,128)} %reshape.7.taps_ref, f32[16,128]{1,0:T(8,128)} %get-tuple-element.6.decay_ref, f32[16,128]{1,0:T(8,128)} %get-tuple-element.5.gain_ref, f32[1,128]{1,0:T(1,128)} %slice.19.skip_ref, bf16[4096,1024]{1,0:T(8,128)(2,1)} %w_hbm.1), custom_call_target="tpu_custom_call" | custom-call | tf_op jit(solution)/shard_map/pallas_call | solution.py:542
  104.4 1.9 %copy.9 = bf16[256,1024]{1,0:T(8,128)(2,1)} copy(bf16[256,1024]{1,0:T(8,128)(2,1)} %shard_map.74) | data formatting | bytes 1048576
  (1 shorter events, 0.0 us)
Async XLA Ops:
  1.6 69.0 %collective-permute-start = (f32[128,42]{0,1:T(8,128)S(1)}, f32[128,42]{0,1:T(8,128)S(1)}, u32[]{:S(2)}, u32[]{:S(2)}) collective-permute-start(f32[128,42]{0,1:T(8,128)S(1)} %fusion.2), channel_id=1, source_target_pairs={{0,0},{1,8},{2,16},{3,24},{4,1},{5,9},{6,17},{7,25},{8,2},{9,10},{... | collective-permute-start | bytes 64520 | tf_op jit(solution)/shard_map/ppermute | solution.py:575
